TPU v7x, 32 devices: a whole 2x2x4 slice. The times are simulated.
32 devices in a mesh: expert: 8 (over z, y), tensor: 4 (over x, core).
Axes of the slice: x: 2, y: 2, z: 4, core: 2. Of those that a mesh axis runs over, the one named last changes fastest.
Arguments:
- inputs: bfloat16 [12608, 512], P('expert'), may hold values from -6 to 6
- gain_attend: float32 [512], replicated, may hold values from 0.25 to 1.75
- triple_weight: bfloat16 [512, 3, 512], P(None, None, 'tensor'), may hold values from -0.25 to 0.25
- project_weight: bfloat16 [512, 512], P('tensor'), may hold values from -1.5 to 1.5
- gain_mixture: float32 [512], replicated, may hold values from 0.25 to 1.75
- router_weight: bfloat16 [512, 16], replicated, may hold values from -0.125 to 0.125
- expert_first: bfloat16 [16, 512, 2048], P('expert', None, 'tensor'), may hold values from -0.25 to 0.25
- expert_second: bfloat16 [16, 2048, 512], P('expert', 'tensor'), may hold values from -0.1875 to 0.1875
- triple_down: bfloat16 [512, 128], replicated, may hold values from -0.25 to 0.25
- triple_up: bfloat16 [128, 3, 512], P(None, None, 'tensor'), may hold values from -1.5 to 1.5
- project_down: bfloat16 [512, 128], P('tensor'), may hold values from -1.5 to 1.5
- project_up: bfloat16 [128, 512], replicated, may hold values from -1.5 to 1.5
- router_down: bfloat16 [512, 128], replicated, may hold values from -0.25 to 0.25
- router_up: bfloat16 [128, 16], replicated, may hold values from -0.75 to 0.75
- first_down: bfloat16 [512, 128], replicated, may hold values from -0.25 to 0.25
- first_up: bfloat16 [128, 2048], P(None, 'tensor'), may hold values from -1.5 to 1.5
- second_down: bfloat16 [2048, 128], P('tensor'), may hold values from -0.1875 to 0.1875
- second_up: bfloat16 [128, 512], replicated, may hold values from -1.5 to 1.5
- adapter_index: int32 [64], P('expert'), may hold values from 0 to 7
- routes: int32 [12608, 2], P('expert'), may hold values from 0 to 15, all different within a row
- priority: int32 [8, 1576], P('expert'), may hold values from 0 to 1575, each once within a row
- cotangent: bfloat16 [12608, 512], P('expert'), may hold values from -6 to 6
Outputs:
- block_output: bfloat16 [12608, 512], P('expert')
- input_grad: bfloat16 [12608, 512], P('expert')
- triple_down_grad: float32 [512, 128], replicated
- triple_up_grad: float32 [128, 3, 512], P(None, None, 'tensor')
- project_down_grad: float32 [512, 128], P('tensor')
- project_up_grad: float32 [128, 512], replicated
- router_down_grad: float32 [512, 128], replicated
- router_up_grad: float32 [128, 16], replicated
- first_down_grad: float32 [512, 128], replicated
- first_up_grad: float32 [128, 2048], P(None, 'tensor')
- second_down_grad: float32 [2048, 128], P('tensor')
- second_up_grad: float32 [128, 512], replicated
Inputs may be any that keep to these rules, and one draw needn't show every extreme that they name: `routes`: each row names 2 different experts. `priority`: each row holds every token index of its group once.
All inputs are finite; a program needn't handle non-finite values.
Results may differ from a plain program's by a relative error of at most 0.028.
Values may be sent and summed in bfloat16 or wider, within the bound.
A program may use at most 192 MiB of HBM per device.

v0:
```python
import jax
import jax.numpy as jnp
from jax import lax
from jax.sharding import PartitionSpec as P

HEAD_DIM = 64
TOP = 2
ADAPTERS = 8
RANK = 16
highest = lax.Precision.HIGHEST
norm_eps = 1e-06


def norm_rows(values, gain):
    centre = jnp.mean(values, axis=-1, keepdims=True)
    shifted = values - centre
    spread = jnp.mean(shifted * shifted, axis=-1, keepdims=True)
    return shifted * lax.rsqrt(spread + norm_eps) * gain


def pick_columns(token_ids):
    column = jnp.arange(ADAPTERS * RANK, dtype=jnp.int32) // RANK
    return (token_ids[:, None] == column[None, :]).astype(jnp.float32)


def place_pairs(route_rows, ranking, capacity, experts):
    count = ranking.shape[0]
    ranked = route_rows[ranking]
    pair_expert = jnp.concatenate([ranked[:, 0], ranked[:, 1]])
    pair_token = jnp.concatenate([ranking, ranking])
    onehot = (pair_expert[:, None] == jnp.arange(experts, dtype=jnp.int32)[None, :]).astype(
        jnp.int32
    )
    position = jnp.sum(jnp.cumsum(onehot, axis=0) * onehot, axis=1) - 1
    kept_pair = position < capacity
    pair_slot = pair_expert * capacity + jnp.minimum(position, capacity - 1)
    target = jnp.where(kept_pair, pair_slot, experts * capacity)
    slot_token = (
        jnp.full((experts * capacity,), count, jnp.int32).at[target].set(pair_token, mode="drop")
    )
    slot_first = jnp.zeros((count,), jnp.int32).at[ranking].set(pair_slot[:count])
    slot_second = jnp.zeros((count,), jnp.int32).at[ranking].set(pair_slot[count:])
    keep_first = jnp.zeros((count,), jnp.int32).at[ranking].set(kept_pair[:count].astype(jnp.int32))
    keep_second = (
        jnp.zeros((count,), jnp.int32).at[ranking].set(kept_pair[count:].astype(jnp.int32))
    )
    return (
        slot_token,
        jnp.stack([slot_first, slot_second], axis=1),
        jnp.stack([keep_first, keep_second], axis=1),
    )


def to_experts(row_block, slot_ids):
    row_block, slot_ids = (
        lax.all_to_all(row_block, "expert", split_axis=0, concat_axis=0, tiled=True),
        lax.all_to_all(slot_ids, "expert", split_axis=0, concat_axis=0, tiled=True),
    )
    return (row_block, slot_ids)


def from_experts(partial_value):
    summed = lax.psum(partial_value.astype(jnp.bfloat16), "tensor")
    row_block = lax.all_to_all(summed, "expert", split_axis=0, concat_axis=0, tiled=True)
    return row_block


def body(
    inputs,
    gain_attend,
    triple_weight,
    project_weight,
    gain_mixture,
    router_weight,
    expert_first,
    expert_second,
    triple_down,
    triple_up,
    project_down,
    project_up,
    router_down,
    router_up,
    first_down,
    first_up,
    second_down,
    second_up,
    adapter_index,
    routes,
    priority,
    cotangent,
):
    f32 = jnp.float32
    bf16 = jnp.bfloat16
    tok_count, model_width = inputs.shape
    images = adapter_index.shape[0]
    seq_len = tok_count // images
    local_heads = triple_weight.shape[2] // HEAD_DIM
    local_width = triple_weight.shape[2]
    tensor_count = lax.axis_size("tensor")
    local_experts = expert_first.shape[0]
    experts = router_weight.shape[1]
    capacity = tensor_count * (
        (5 * tok_count * TOP + 4 * tensor_count * experts - 1) // (4 * tensor_count * experts)
    )
    score_scale = HEAD_DIM ** (-0.5)
    adapt_width = ADAPTERS * RANK
    token_ids = jnp.repeat(adapter_index, seq_len, total_repeat_length=tok_count)
    pick_cols = pick_columns(token_ids)
    source = inputs.astype(f32)
    normed1, norm1_back = jax.vjp(lambda values: norm_rows(values, gain_attend), source)
    attn_in = normed1.astype(bf16)
    triple_flat = triple_weight.reshape(model_width, 3 * local_width)
    triple_high = triple_up.reshape(adapt_width, 3 * local_width)
    triple_low = (jnp.dot(attn_in, triple_down, preferred_element_type=f32) * pick_cols).astype(
        bf16
    )
    triple = jnp.dot(attn_in, triple_flat, preferred_element_type=f32) + jnp.dot(
        triple_low, triple_high, preferred_element_type=f32
    )
    triple = triple.astype(bf16).reshape(images, seq_len, 3, local_heads, HEAD_DIM)
    queries = triple[:, :, 0]
    key_rows = triple[:, :, 1]
    value_rows = triple[:, :, 2]
    scores = (
        jnp.einsum("bqhd,bkhd->bhqk", queries, key_rows, preferred_element_type=f32) * score_scale
    )
    row_max = jnp.max(scores, axis=-1, keepdims=True)
    shifted = jnp.exp(scores - row_max)
    row_total = jnp.sum(shifted, axis=-1, keepdims=True)
    log_total = row_max + jnp.log(row_total)
    probs = (shifted / row_total).astype(bf16)
    attended = (
        jnp.einsum("bhqk,bkhd->bqhd", probs, value_rows, preferred_element_type=f32)
        .reshape(tok_count, local_width)
        .astype(bf16)
    )
    branch_part = jnp.dot(attended, project_weight, preferred_element_type=f32)
    project_part = jnp.dot(attended, project_down, preferred_element_type=f32)
    branch_sum, project_sum = (
        lax.psum(branch_part.astype(jnp.bfloat16), "tensor").astype(jnp.float32),
        lax.psum(project_part.astype(jnp.bfloat16), "tensor").astype(jnp.float32),
    )
    project_low = (project_sum * pick_cols).astype(bf16)
    middle = source + branch_sum + jnp.dot(project_low, project_up, preferred_element_type=f32)
    normed2, norm2_back = jax.vjp(lambda values: norm_rows(values, gain_mixture), middle)
    mixed_in = normed2.astype(bf16)
    router_low = jnp.dot(mixed_in, router_down, preferred_element_type=f32) * pick_cols
    logits = jnp.dot(mixed_in, router_weight, preferred_element_type=f32) + jnp.dot(
        router_low, router_up.astype(f32), precision=highest
    )
    chosen = (routes[:, :, None] == jnp.arange(experts, dtype=jnp.int32)[None, None, :]).astype(f32)
    picked = jnp.sum(chosen * logits[:, None, :], axis=-1)
    gate_prob = jax.nn.softmax(picked, axis=-1)
    slot_token, slot_pairs, keep_pairs = place_pairs(routes, priority[0], capacity, experts)
    keep_float = keep_pairs.astype(f32)
    gate_wts = gate_prob * keep_float
    padded = jnp.concatenate([mixed_in, jnp.zeros((1, model_width), bf16)], axis=0)
    send_rows = padded[slot_token].reshape(experts, capacity, model_width)
    id_pad = jnp.concatenate([token_ids, jnp.zeros((1,), jnp.int32)])
    send_ids = id_pad[slot_token].reshape(experts, capacity)
    got_rows, got_ids = to_experts(send_rows, send_ids)
    sources = got_rows.shape[0] // local_experts
    got = got_rows.reshape(sources, local_experts, capacity, model_width)
    got_cols = pick_columns(got_ids.reshape(-1)).reshape(
        sources, local_experts, capacity, adapt_width
    )
    first_low = (
        jnp.einsum("necd,dr->necr", got, first_down, preferred_element_type=f32) * got_cols
    ).astype(bf16)
    pre = jnp.einsum("necd,edf->necf", got, expert_first, preferred_element_type=f32) + jnp.einsum(
        "necr,rf->necf", first_low, first_up, preferred_element_type=f32
    )
    hidden_val, gelu_back = jax.vjp(lambda values: jax.nn.gelu(values, approximate=False), pre)
    hidden = hidden_val.astype(bf16)
    second_low = (
        jnp.einsum("necf,fr->necr", hidden, second_down, preferred_element_type=f32) * got_cols
    ).astype(bf16)
    part_out = jnp.einsum(
        "necf,efd->necd", hidden, expert_second, preferred_element_type=f32
    ) + jnp.einsum("necr,rd->necd", second_low, second_up, preferred_element_type=f32)
    back_rows = from_experts(part_out.reshape(sources * local_experts, capacity, model_width))
    flat_rows = back_rows.reshape(experts * capacity, model_width)
    fetched = flat_rows[slot_pairs].astype(f32)
    block_output = (middle + jnp.sum(gate_wts[:, :, None] * fetched, axis=1)).astype(bf16)
    grad_out = cotangent.astype(f32)
    grad_gate = jnp.sum(fetched * grad_out[:, None, :], axis=-1) * keep_float
    pair_target = jnp.where(keep_pairs > 0, slot_pairs, experts * capacity)
    slot_gate = jnp.zeros((experts * capacity,), f32).at[pair_target].set(gate_wts, mode="drop")
    grad_pad = jnp.concatenate([cotangent, jnp.zeros((1, model_width), bf16)], axis=0)
    slot_grad = (
        (grad_pad[slot_token].astype(f32) * slot_gate[:, None])
        .astype(bf16)
        .reshape(experts, capacity, model_width)
    )
    got_grad, grad_ids = to_experts(slot_grad, send_ids)
    grad_res = got_grad.reshape(sources, local_experts, capacity, model_width)
    grad_cols = pick_columns(grad_ids.reshape(-1)).reshape(
        sources, local_experts, capacity, adapt_width
    )
    res_low = (
        jnp.einsum("necd,rd->necr", grad_res, second_up, preferred_element_type=f32) * grad_cols
    ).astype(bf16)
    grad_hidden = jnp.einsum(
        "necd,efd->necf", grad_res, expert_second, preferred_element_type=f32
    ) + jnp.einsum("necr,fr->necf", res_low, second_down, preferred_element_type=f32)
    grad_pre = gelu_back(grad_hidden)[0].astype(bf16)
    second_up_part = jnp.einsum("necr,necd->rd", second_low, grad_res, preferred_element_type=f32)
    second_down_part = jnp.einsum("necf,necr->fr", hidden, res_low, preferred_element_type=f32)
    first_up_part = jnp.einsum("necr,necf->rf", first_low, grad_pre, preferred_element_type=f32)
    pre_low = (
        jnp.einsum("necf,rf->necr", grad_pre, first_up, preferred_element_type=f32) * grad_cols
    ).astype(bf16)
    first_down_part = jnp.einsum("necd,necr->dr", got, pre_low, preferred_element_type=f32)
    grad_got = jnp.einsum(
        "necf,edf->necd", grad_pre, expert_first, preferred_element_type=f32
    ) + jnp.einsum("necr,dr->necd", pre_low, first_down, preferred_element_type=f32)
    back_grad = from_experts(grad_got.reshape(sources * local_experts, capacity, model_width))
    back_flat = back_grad.reshape(experts * capacity, model_width)
    grad_mixed = jnp.sum(back_flat[slot_pairs].astype(f32) * keep_float[:, :, None], axis=1)
    grad_picked = gate_prob * (grad_gate - jnp.sum(gate_prob * grad_gate, axis=-1, keepdims=True))
    grad_logits = jnp.sum(chosen * grad_picked[:, :, None], axis=1)
    logit_low = jnp.dot(grad_logits, router_up.astype(f32).T, precision=highest) * pick_cols
    grad_mixed = (
        grad_mixed
        + jnp.dot(grad_logits, router_weight.astype(f32).T, precision=highest)
        + jnp.dot(logit_low, router_down.astype(f32).T, precision=highest)
    )
    router_up_part = jnp.dot(router_low.T, grad_logits, precision=highest)
    router_down_part = jnp.dot(mixed_in.astype(f32).T, logit_low, precision=highest)
    grad_middle = grad_out + norm2_back(grad_mixed)[0]
    grad_branch = grad_middle.astype(bf16)
    project_up_part = jnp.dot(project_low.T, grad_branch, preferred_element_type=f32)
    branch_low = (
        jnp.dot(grad_branch, project_up.T, preferred_element_type=f32) * pick_cols
    ).astype(bf16)
    project_down_part = jnp.dot(attended.T, branch_low, preferred_element_type=f32)
    grad_attended = (
        jnp.dot(grad_branch, project_weight.T, preferred_element_type=f32)
        + jnp.dot(branch_low, project_down.T, preferred_element_type=f32)
    ).astype(bf16)
    grad_heads = grad_attended.reshape(images, seq_len, local_heads, HEAD_DIM)
    again = (
        jnp.einsum("bqhd,bkhd->bhqk", queries, key_rows, preferred_element_type=f32) * score_scale
    )
    probs_again = jnp.exp(again - log_total)
    grad_probs = jnp.einsum("bqhd,bkhd->bhqk", grad_heads, value_rows, preferred_element_type=f32)
    grad_values = jnp.einsum(
        "bhqk,bqhd->bkhd", probs_again.astype(bf16), grad_heads, preferred_element_type=f32
    )
    inner = jnp.sum(probs_again * grad_probs, axis=-1, keepdims=True)
    grad_scores = (probs_again * (grad_probs - inner)).astype(bf16)
    grad_queries = (
        jnp.einsum("bhqk,bkhd->bqhd", grad_scores, key_rows, preferred_element_type=f32)
        * score_scale
    )
    grad_keys = (
        jnp.einsum("bhqk,bqhd->bkhd", grad_scores, queries, preferred_element_type=f32)
        * score_scale
    )
    grad_triple = (
        jnp.stack([grad_queries, grad_keys, grad_values], axis=2)
        .reshape(tok_count, 3 * local_width)
        .astype(bf16)
    )
    triple_up_part = jnp.dot(triple_low.T, grad_triple, preferred_element_type=f32).reshape(
        adapt_width, 3, local_width
    )
    triple_grad_low = jnp.dot(grad_triple, triple_high.T, preferred_element_type=f32) * pick_cols
    triple_down_part = jnp.dot(attn_in.T, triple_grad_low.astype(bf16), preferred_element_type=f32)
    grad_in_part = jnp.dot(grad_triple, triple_flat.T, preferred_element_type=f32) + jnp.dot(
        triple_grad_low.astype(bf16), triple_down.T, preferred_element_type=f32
    )
    grad_attn_in = lax.psum(grad_in_part.astype(jnp.bfloat16), "tensor").astype(jnp.float32)
    input_grad = (grad_middle + norm1_back(grad_attn_in)[0]).astype(bf16)
    (
        triple_up_grad,
        project_down_grad,
        project_up_grad,
        router_down_grad,
        router_up_grad,
        first_up_grad,
        second_down_grad,
    ) = lax.psum(
        (
            triple_up_part,
            project_down_part,
            project_up_part,
            router_down_part,
            router_up_part,
            first_up_part,
            second_down_part,
        ),
        "expert",
    )
    triple_down_grad, first_down_grad, second_up_grad = lax.psum(
        (triple_down_part, first_down_part, second_up_part), ("expert", "tensor")
    )
    return (
        block_output,
        input_grad,
        triple_down_grad,
        triple_up_grad,
        project_down_grad,
        project_up_grad,
        router_down_grad,
        router_up_grad,
        first_down_grad,
        first_up_grad,
        second_down_grad,
        second_up_grad,
    )


def solution(mesh):
    return jax.shard_map(
        body,
        mesh=mesh,
        in_specs=(
            P("expert", None),
            P(),
            P(None, None, "tensor"),
            P("tensor", None),
            P(),
            P(),
            P("expert", None, "tensor"),
            P("expert", "tensor", None),
            P(),
            P(None, None, "tensor"),
            P("tensor", None),
            P(),
            P(),
            P(),
            P(),
            P(None, "tensor"),
            P("tensor", None),
            P(),
            P("expert"),
            P("expert", None),
            P("expert", None),
            P("expert", None),
        ),
        out_specs=(
            P("expert", None),
            P("expert", None),
            P(),
            P(None, None, "tensor"),
            P("tensor", None),
            P(),
            P(),
            P(),
            P(),
            P(None, "tensor"),
            P("tensor", None),
            P(),
        ),
        check_vma=False,
    )
```

profile of v0, /device:TPU:0, one launch (start us, length us, event | category | flops | bytes accessed | tf_op | source)
XLA Modules:
  0.0 1132.3 jit_solution(9242527268222042039)
XLA Ops:
  16.5 5.2 select_select_fusion
  24.7 4.6 reshape.747
  47.3 3.2 gather_fusion
  51.4 4.6 reduce-window.14
  57.8 8.8 scatter_custom_fusion.3
  66.6 8.8 scatter_custom_fusion.4
  75.4 9.0 scatter_custom_fusion
  84.5 8.8 scatter_custom_fusion.1
  99.0 15.8 %scatter_custom_fusion.2 = s32[3968]{0:T(1024)S(1)} fusion(s32[3152]{0:T(1024)S(1)} %fusion.105, s32[3152]{0:T(1024)S(1)} %pad_add_fusion.1, s32[]{:T(128)} %constant.191.clone.1), kind=kCustom, calls=%fused_computation.210 | custom fusion | bytes 15876 | tf_op jit(solution)/shard_map/scatter | solution.py:39
  114.9 12.4 %gather_fusion.4 = bf16[3968,512]{1,0:T(8,128)(2,1)} fusion(bf16[1577,512]{1,0:T(8,128)(2,1)S(1)} %concatenate.76, s32[4096]{0:T(1024)S(1)} %pad_clamp_fusion.1), kind=kCustom, calls=%fused_computation.4 | custom fusion | bytes 8142336 | tf_op jit(solution)/shard_map/gather | solution.py:191
  127.3 2.9 fusion.136
  136.4 16.0 %scatter_custom_fusion.5 = f32[3968]{0:T(1024)S(1)} fusion(s32[3152]{0:T(1024)} %reshape.722, f32[3152]{0:T(1024)S(1)} %reshape.724, f32[]{:T(128)} %constant.180.clone.1), kind=kCustom, calls=%fused_computation.208 | custom fusion | bytes 16384 | tf_op jit(solution)/shard_map/scatter | solution.py:188
  152.5 4.0 fusion.1
  156.5 7.7 all-to-all-start.3
  165.8 12.4 %gather_fusion.1 = bf16[3968,512]{1,0:T(8,128)(2,1)} fusion(bf16[1577,512]{1,0:T(8,128)(2,1)S(1)} %concatenate.72, s32[4096]{0:T(1024)S(1)} %pad_clamp_fusion.1), kind=kCustom, calls=%fused_computation.1 | custom fusion | bytes 8142336 | tf_op jit(solution)/shard_map/gather | solution.py:158
  178.2 76.5 %all-to-all-done.3 = bf16[16,248,512]{2,1,0:T(8,128)(2,1)} async-done(((bf16[16,248,512]{2,1,0:T(8,128)(2,1)}), bf16[16,248,512]{2,1,0:T(8,128)(2,1)}, u32[]{:S(2)}, u32[]{:S(2)}) %all-to-all-start.3) | async-done | bytes 4063264 | tf_op jit(solution)/shard_map/all_to_all | solution.py:56
  254.7 4.6 all-to-all-start
  259.3 20.9 %gather_fusion.2 = s32[3968]{0:T(1024)S(1)} fusion(s32[1577]{0:T(1024)S(1)} %pad_add_fusion.2, s32[4096]{0:T(1024)S(1)} %pad_clamp_fusion.1), kind=kCustom, calls=%fused_computation.2 | custom fusion | bytes 47616 | tf_op jit(solution)/shard_map/gather | solution.py:160
  280.9 7.6 fusion.19
  288.5 60.5 %all-to-all-done = bf16[16,248,512]{2,1,0:T(8,128)(2,1)} async-done(((bf16[16,248,512]{2,1,0:T(8,128)(2,1)}), bf16[16,248,512]{2,1,0:T(8,128)(2,1)}, u32[]{:S(2)}, u32[]{:S(2)}) %all-to-all-start) | async-done | bytes 4063264 | tf_op jit(solution)/shard_map/all_to_all | solution.py:56
  349.0 3.6 all-to-all-start.1
  352.7 7.6 fusion.23
  360.3 3.4 fusion.39
  363.8 6.7 fusion.44
  370.5 19.2 %multiply_convert_fusion = (bf16[8,2,248,512]{3,2,0,1:T(8,128)(2,1)S(1)}, f32[8,2,248,512]{3,2,0,1:T(8,128)}) fusion(f32[8,2,248,512]{3,2,0,1:T(8,128)S(1)} %get-tuple-element.75, u8[2,248,512]{2,1,0:T(8,128)(4,1)S(1)} %get-tuple-element.25, u8[2,248,512]{2,1,0:T(8,128)(4,1)S(1)} %get-tuple-element.24), kind=kLoop, calls=%fused_computation.28 | loop fusion | flops 142213120 | bytes 20824064 | tf_op jit(solution)/shard_map/convert_element_type | solution.py:174
  389.8 4.9 fusion.41
  394.7 8.2 add_convert_fusion
  418.1 150.5 %all-reduce.19.cloned.1.call-done = (bf16[16,248,512]{2,1,0:T(8,128)(2,1)}, bf16[16,248,512]{2,1,0:T(8,128)(2,1)}) async-done(((bf16[16,248,512]{2,1,0:T(8,128)(2,1)}, bf16[16,248,512]{2,1,0:T(8,128)(2,1)}), (bf16[16,248,512]{2,1,0:T(8,128)(2,1)}, bf16[16,248,512]{2,1,0:T(8,128)(2,1)})) %all-reduce.19.cloned.1.call-update) | async-done | bytes 8126480 | tf_op jit(solution)/shard_map/psum | solution.py:63
  568.7 96.2 %all_to_all.30 = bf16[16,248,512]{2,1,0:T(8,128)(2,1)} all-to-all(bf16[16,248,512]{2,1,0:T(8,128)(2,1)} %get-tuple-element.39), channel_id=1, replica_groups=mesh['expert'=8,'tensor'=4] {'expert'}, dimensions={0} | all-to-all | bytes 8126464 | tf_op jit(solution)/shard_map/all_to_all | solution.py:64
  664.9 4.7 all-to-all-start.4
  672.9 4.1 convolution_bitcast_fusion.1
  679.0 3.7 fusion.64
  682.7 4.1 fusion.61
  686.8 13.5 %gather_fusion.3 = bf16[3152,512]{1,0:T(8,128)(2,1)} fusion(bf16[3968,512]{1,0:T(8,128)(2,1)} %bitcast.214, s32[4096]{0:T(1024)S(1)} %pad_clamp_fusion), kind=kCustom, calls=%fused_computation.3 | custom fusion | bytes 6467904 | tf_op jit(solution)/shard_map/gather | solution.py:183
  700.3 7.9 reshape.734
  708.2 21.8 %multiply_reduce_fusion = (f32[1576,2]{1,0:T(8,128)}, f32[1576,512]{1,0:T(8,128)}) fusion(f32[1576,2,512]{2,1,0:T(2,128)} %reshape.734, f32[1576,512]{1,0:T(8,128)} %convert_element_type.195, f32[1576,2]{1,0:T(8,128)S(1)} %copy.191), kind=kLoop, calls=%fused_computation.41 | loop fusion | flops 5645232 | bytes 12935808 | tf_op jit(solution)/shard_map/reduce_sum | solution.py:186
  731.5 27.1 %all-to-all-done.4 = bf16[16,248,512]{2,1,0:T(8,128)(2,1)} async-done(((bf16[16,248,512]{2,1,0:T(8,128)(2,1)}), bf16[16,248,512]{2,1,0:T(8,128)(2,1)}, u32[]{:S(2)}, u32[]{:S(2)}) %all-to-all-start.4) | async-done | bytes 4063264 | tf_op jit(solution)/shard_map/all_to_all | solution.py:64
  758.7 13.1 %gather_fusion.5 = bf16[3152,512]{1,0:T(8,128)(2,1)} fusion(bf16[3968,512]{1,0:T(8,128)(2,1)} %bitcast.41, s32[4096]{0:T(1024)S(1)} %pad_clamp_fusion), kind=kCustom, calls=%fused_computation.5 | custom fusion | bytes 6467904 | tf_op jit(solution)/shard_map/gather | solution.py:219
  771.8 7.9 reshape.735
  780.6 35.1 %multiply_reduce_fusion.1 = f32[1576,512]{1,0:T(8,128)S(1)} fusion(f32[1576,2,512]{2,1,0:T(2,128)} %reshape.735, f32[1576,2]{1,0:T(8,128)S(1)} %copy.207), kind=kLoop, calls=%fused_computation.42 | loop fusion | flops 2420736 | bytes 9695552 | tf_op jit(solution)/shard_map/reduce_sum | solution.py:219
  827.2 3.1 multiply_reduce_fusion.3
  835.6 3.1 convert_element_type.211
  846.7 3.3 fusion.102
  850.9 20.3 %psum.115 = f32[128,16]{0,1:T(8,128)} all-reduce(f32[128,16]{0,1:T(8,128)S(1)} %fusion.144), channel_id=1, replica_groups=mesh['expert'=8,'tensor'=4] {'expert'}, use_global_device_ids=true, to_apply=%region_38.39 | all-reduce | flops 2048 | bytes 16384 | tf_op jit(solution)/shard_map/psum | solution.py:283
  871.2 4.3 fusion.143
  875.6 10.3 all-reduce.13.cloned.1.call-done
  894.2 127.9 %all-reduce.15.cloned.1.call-done = (f32[512,128]{1,0:T(8,128)}, f32[512,128]{1,0:T(8,128)}, f32[128,512]{1,0:T(8,128)}) async-done(((f32[512,128]{1,0:T(8,128)}, f32[512,128]{1,0:T(8,128)}, f32[128,512]{1,0:T(8,128)}), (f32[512,128]{1,0:T(8,128)}, f32[512,128]{1,0:T(8,128)}, f32[128,512]{1,0:T(8,128)})) %all-reduce.15.cloned.1.call-update) | async-done | bytes 786448 | tf_op jit(solution)/shard_map/psum | solution.py:295
  1022.1 90.5 %all-reduce.17.cloned.1.call-done = (f32[128,3,128]{2,0,1:T(8,128)}, f32[128,128]{1,0:T(8,128)}, f32[128,512]{1,0:T(8,128)}, f32[512,128]{1,0:T(8,128)}, f32[128,512]{1,0:T(8,128)}, /*index=5*/f32[512,128]{1,0:T(8,128)}) async-done(((f32[128,3,128]{2,0,1:T(8,128)}, f32[128,128]{1,0:T(8,128)}, f32[128,512]{1,0:T(8,128)}, f32[512,128]{1,0:T(8,128)}, f32[128,512]{1,0:T(8,128)}, ...) | async-done | bytes 1310736 | tf_op jit(solution)/shard_map/psum | solution.py:283
  (358 shorter events, 116.0 us)
Async XLA Ops:
  7.2 345.5 %copy-start = (bf16[2,512,512]{2,1,0:T(8,128)(2,1)S(1)}, bf16[2,512,512]{2,1,0:T(8,128)(2,1)}, u32[]{:S(2)}) copy-start(bf16[2,512,512]{2,1,0:T(8,128)(2,1)} %param.30) | copy-start | bytes 3145732
  7.2 7.5 copy-start.6
  7.2 6.1 copy-start.51
  7.2 7.4 copy-start.83
  7.2 120.1 %all-reduce.21.cloned.1.call-start = ((), (), s32[]{:S(2)}) async-start(), calls=%async_computation.9 | async-start | bytes 4034560 | tf_op jit(solution)/shard_map/psum | solution.py:140
  7.3 14.4 %copy-start.89 = (s32[128]{0:T(128)}, s32[128]{0:T(128)S(1)}, u32[]{:S(2)}) copy-start(s32[128]{0:T(128)S(1)} %and_select_fusion) | copy-start | bytes 1540
  10.6 5.8 copy-start.54
  14.7 7.7 copy-start.52
  15.3 6.4 copy-start.9
  15.4 6.4 copy-start.63
  34.4 6.1 copy-start.26
  114.9 12.4 %copy-start.67 = (bf16[128,512]{1,0:T(8,128)(2,1)S(1)}, bf16[128,512]{1,0:T(8,128)(2,1)}, u32[]{:S(2)}) copy-start(bf16[128,512]{1,0:T(8,128)(2,1)} %param.35) | copy-start | bytes 393220
  114.9 12.4 %copy-start.90 = (s32[128]{0:T(128)S(1)}, s32[128]{0:T(128)}, u32[]{:S(2)}) copy-start(s32[128]{0:T(128)} %copy-done.89) | copy-start | bytes 1540
  156.5 98.1 %all-to-all-start.3 = ((bf16[16,248,512]{2,1,0:T(8,128)(2,1)}), bf16[16,248,512]{2,1,0:T(8,128)(2,1)}, u32[]{:S(2)}, u32[]{:S(2)}) async-start(bf16[16,248,512]{2,1,0:T(8,128)(2,1)} %fusion.1), calls=%async_computation.3 | async-start | bytes 8126464 | tf_op jit(solution)/shard_map/all_to_all | solution.py:56
  254.7 94.3 %all-to-all-start = ((bf16[16,248,512]{2,1,0:T(8,128)(2,1)}), bf16[16,248,512]{2,1,0:T(8,128)(2,1)}, u32[]{:S(2)}, u32[]{:S(2)}) async-start(bf16[16,248,512]{2,1,0:T(8,128)(2,1)} %bitcast.219), calls=%async_computation | async-start | bytes 8126464 | tf_op jit(solution)/shard_map/all_to_all | solution.py:56
  259.3 21.6 %copy-start.30 = (bf16[2,512,512]{2,1,0:T(8,128)(2,1)S(1)}, bf16[2,512,512]{2,1,0:T(8,128)(2,1)}, u32[]{:S(2)}) copy-start(bf16[2,512,512]{2,1,0:T(8,128)(2,1)} %param.31) | copy-start | bytes 3145732
  349.0 11.3 all-to-all-start.1
  352.6 216.0 %all-reduce.19.cloned.1.call-start = ((), (), s32[]{:S(2)}) async-start(), calls=%async_computation.8 | async-start | bytes 16252928 | tf_op jit(solution)/shard_map/psum | solution.py:63
  352.7 7.6 copy-start.58
  352.7 7.6 copy-start.91
  363.7 6.8 copy-start.42
  363.8 30.9 %slice-start = ((s8[8126464]{0:T(1024)(128)(4,1)}), s8[4194304]{0:T(1024)(128)(4,1)S(1)}, s32[]{:S(2)}) async-start(s8[8126464]{0:T(1024)(128)(4,1)} %bitcast.220), calls=%async_computation.10 | async-start | bytes 8388608
  370.5 19.2 %copy-start.21 = (f32[8,2,248,512]{3,2,0,1:T(8,128)}, f32[8,2,248,512]{3,2,0,1:T(8,128)S(1)}, u32[]{:S(2)}) copy-start(f32[8,2,248,512]{3,2,0,1:T(8,128)S(1)} %get-tuple-element.75) | copy-start | bytes 24379396
  370.5 19.2 %copy-start.60 = (bf16[128,512]{1,0:T(8,128)(2,1)S(1)}, bf16[128,512]{1,0:T(8,128)(2,1)}, u32[]{:S(2)}) copy-start(bf16[128,512]{1,0:T(8,128)(2,1)} %param.41) | copy-start | bytes 393220
  370.5 24.1 %slice-start.1 = ((s8[8126464]{0:T(1024)(128)(4,1)}), s8[3932160]{0:T(1024)(128)(4,1)S(1)}, s32[]{:S(2)}) async-start(s8[8126464]{0:T(1024)(128)(4,1)} %bitcast.220), calls=%async_computation.11 | async-start | bytes 7864320
  389.8 23.2 %copy-start.15 = (bf16[8,2,248,512]{3,2,0,1:T(8,128)(2,1)}, bf16[8,2,248,512]{3,2,0,1:T(8,128)(2,1)S(1)}, u32[]{:S(2)}) copy-start(bf16[8,2,248,512]{3,2,0,1:T(8,128)(2,1)S(1)} %get-tuple-element.47) | copy-start | bytes 12189700
  394.6 8.2 copy-start.102
  664.9 93.8 %all-to-all-start.4 = ((bf16[16,248,512]{2,1,0:T(8,128)(2,1)}), bf16[16,248,512]{2,1,0:T(8,128)(2,1)}, u32[]{:S(2)}, u32[]{:S(2)}) async-start(bf16[16,248,512]{2,1,0:T(8,128)(2,1)} %get-tuple-element.40), calls=%async_computation.4 | async-start | bytes 8126464 | tf_op jit(solution)/shard_map/all_to_all | solution.py:64
  669.6 216.3 %all-reduce.13.cloned.1.call-start = ((), (), s32[]{:S(2)}) async-start(), calls=%async_computation.5 | async-start | bytes 3227648 | tf_op jit(solution)/shard_map/psum | solution.py:273
  708.2 23.2 %copy-start.72 = (f32[1576,2]{0,1:T(2,128)S(1)}, f32[1576,2]{0,1:T(2,128)}, u32[]{:S(2)}) copy-start(f32[1576,2]{0,1:T(2,128)} %get-tuple-element.46) | copy-start | bytes 37828
  708.2 23.3 %copy-start.71 = (s32[1576,2]{0,1:T(2,128)S(1)}, s32[1576,2]{0,1:T(2,128)}, u32[]{:S(2)}) copy-start(s32[1576,2]{0,1:T(2,128)} %param.43) | copy-start | bytes 37828
  731.5 84.2 %copy-start.35 = (f32[1576,16]{0,1:T(8,128)}, f32[1576,16]{0,1:T(8,128)S(1)}, u32[]{:S(2)}) copy-start(f32[1576,16]{0,1:T(8,128)S(1)} %select_reduce_fusion) | copy-start | bytes 302596
  771.8 7.9 copy-start.92
  780.6 35.1 %copy-start.78 = (bf16[512,16]{0,1:T(8,128)(2,1)S(1)}, bf16[512,16]{0,1:T(8,128)(2,1)}, u32[]{:S(2)}) copy-start(bf16[512,16]{0,1:T(8,128)(2,1)} %param.29) | copy-start | bytes 49156
  833.5 5.8 copy-start.32
  843.6 178.5 %all-reduce.15.cloned.1.call-start = ((), (), s32[]{:S(2)}) async-start(), calls=%async_computation.6 | async-start | bytes 1572864 | tf_op jit(solution)/shard_map/psum | solution.py:295
  844.2 5.8 copy-start.25
  844.2 5.8 copy-start.40
  850.0 36.0 %copy-start.7 = (bf16[1576,512]{1,0:T(8,128)(2,1)S(1)}, bf16[1576,512]{1,0:T(8,128)(2,1)}, u32[]{:S(2)}) copy-start(bf16[1576,512]{1,0:T(8,128)(2,1)} %param.24) | copy-start | bytes 4841476
  850.0 36.0 %copy-start.55 = (f32[1576]{0:T(1024)S(1)}, f32[1576]{0:T(1024)}, u32[]{:S(2)}) copy-start(f32[1576]{0:T(1024)} %copy-done.54) | copy-start | bytes 18916
  850.0 36.0 %copy-start.84 = (f32[512]{0:T(512)S(1)}, f32[512]{0:T(512)}, u32[]{:S(2)}) copy-start(f32[512]{0:T(512)} %param.25) | copy-start | bytes 6148
  850.0 262.7 %all-reduce.17.cloned.1.call-start = ((), (), s32[]{:S(2)}) async-start(), calls=%async_computation.7 | async-start | bytes 2621440 | tf_op jit(solution)/shard_map/psum | solution.py:283
  871.2 17.2 %copy-start.74 = (f32[1576]{0:T(1024)S(1)}, f32[1576]{0:T(1024)}, u32[]{:S(2)}) copy-start(f32[1576]{0:T(1024)} %copy-done.73) | copy-start | bytes 18916
  871.2 17.2 %copy-start.62 = (f32[1576]{0:T(1024)S(1)}, f32[1576]{0:T(1024)}, u32[]{:S(2)}) copy-start(f32[1576]{0:T(1024)} %copy-done.61) | copy-start | bytes 18916
  885.9 5.4 copy-start.14
  891.4 234.2 %copy-start.1 = (bf16[2,512,512]{2,1,0:T(8,128)(2,1)S(1)}, bf16[2,512,512]{2,1,0:T(8,128)(2,1)}, u32[]{:S(2)}) copy-start(bf16[2,512,512]{2,1,0:T(8,128)(2,1)} %param.30) | copy-start | bytes 3145732
  1022.1 102.7 %copy-start.56 = (f32[128,512]{1,0:T(8,128)S(1)}, f32[128,512]{1,0:T(8,128)}, u32[]{:S(2)}) copy-start(f32[128,512]{1,0:T(8,128)} %get-tuple-element.91) | copy-start | bytes 786436
  1112.6 11.5 %copy-start.57 = (f32[512,128]{1,0:T(8,128)S(1)}, f32[512,128]{1,0:T(8,128)}, u32[]{:S(2)}) copy-start(f32[512,128]{1,0:T(8,128)} %get-tuple-element.90) | copy-start | bytes 786436
  (67 other events, 155.5 us)
Sparse Core Ops, SparseCore 0:
  47.1 53.1 all-reduce.20
  418.3 150.3 all-reduce.18
  843.7 42.1 all-reduce.12
  891.9 130.2 all-reduce.14
  1028.0 84.5 all-reduce.16
where the time goes:
time: 1140 us; the launch traced here: 1130 us
  waiting for transfers between devices  543 us (48%)
  local copies, waits for them, and re-layouts  219 us (19%)
  blocking collectives  117 us (10%)
  other arithmetic  114 us (10%)
  matrix products  102 us (9%)
  starting transfers between devices  20.8 us (2%)
  between operations  15.9 us (1%)
    psum x1, waiting for transfers between devices, from_experts(): summed = lax.psum(partial_value.astype(jnp.bfloat16), 'tensor')  151 us
    all_to_all x2, waiting for transfers between devices, to_experts(): lax.all_to_all(row_block, 'expert', split_axis=0, concat_axis=0, tiled=True)  137 us
    psum x1, waiting for transfers between devices, body(): lax.psum((triple_down_part, first_down_part, second_up_part), ('expert',...  128 us
    all_to_all x1, blocking collectives, from_experts(): lax.all_to_all(summed, 'expert', split_axis=0, concat_axis=0, tiled=True)  96.2 us
    psum x1, waiting for transfers between devices, body(): lax.psum((triple_up_part, project_down_part, project_up_part, router_down...  90.5 us
    reduce_sum x1, other arithmetic, body(): jnp.sum(back_flat[slot_pairs].astype(f32) * keep_float[:, :, None], axis=1)  35.1 us
    unnamed x229, local copies, waits for them, and re-layouts  28.4 us
    all_to_all x1, waiting for transfers between devices, from_experts(): lax.all_to_all(summed, 'expert', split_axis=0, concat_axis=0, tiled=True)  27.1 us
  transfers between devices with their start and end apart: 9, of which 7 were waited for; matrix products, arithmetic and copies ran while one was open for 19% of the time, Pallas kernels for 0%

commit v1 on v0

--- a/solution.py
+++ b/solution.py
@@ -293,7 +293,7 @@
         "expert",
     )
     triple_down_grad, first_down_grad, second_up_grad = lax.psum(
-        (triple_down_part, first_down_part, second_up_part), ("expert", "tensor")
+        lax.psum((triple_down_part, first_down_part, second_up_part), "tensor"), "expert"
     )
     return (
         block_output,

time: 1140 us -> 1060 us (0.930)
  waiting for transfers between devices: 543 us -> 462 us
    psum x2, waiting for transfers between devices: 218 us -> 124 us  [the longest x1 104 us: body(): lax.psum(lax.psum((triple_down_part, first_down_part, second_up_part), 't...]
    psum x1, waiting for transfers between devices: 10.3 us -> 23.3 us  [body(): lax.psum(grad_in_part.astype(jnp.bfloat16), 'tensor').astype(jnp.float32)]
    unnamed x229 -> x231, local copies, waits for them, and re-layouts: 28.4 us -> 28.3 us
  transfers between devices with their start and end apart: 9 -> 9, of which waited for: 7 -> 7; matrix products, arithmetic and copies ran while one was open for 19% -> 20% of each run, Pallas kernels for 0% -> 0%
where the time goes in v1:
time: 1060 us; the launch traced here: 1050 us
  waiting for transfers between devices  462 us (44%)
  local copies, waits for them, and re-layouts  219 us (21%)
  blocking collectives  119 us (11%)
  other arithmetic  114 us (11%)
  matrix products  105 us (10%)
  starting transfers between devices  20.8 us (2%)
  between operations  15.9 us (2%)
    psum x1, waiting for transfers between devices, from_experts(): summed = lax.psum(partial_value.astype(jnp.bfloat16), 'tensor')  151 us
    all_to_all x2, waiting for transfers between devices, to_experts(): lax.all_to_all(row_block, 'expert', split_axis=0, concat_axis=0, tiled=True)  137 us
    psum x1, waiting for transfers between devices, body(): lax.psum(lax.psum((triple_down_part, first_down_part, second_up_part), 't...  104 us
    all_to_all x1, blocking collectives, from_experts(): lax.all_to_all(summed, 'expert', split_axis=0, concat_axis=0, tiled=True)  96.2 us
    reduce_sum x1, other arithmetic, body(): jnp.sum(back_flat[slot_pairs].astype(f32) * keep_float[:, :, None], axis=1)  35.1 us
    unnamed x231, local copies, waits for them, and re-layouts  28.3 us
    all_to_all x1, waiting for transfers between devices, from_experts(): lax.all_to_all(summed, 'expert', split_axis=0, concat_axis=0, tiled=True)  27.2 us
    psum x1, waiting for transfers between devices, body(): lax.psum(grad_in_part.astype(jnp.bfloat16), 'tensor').astype(jnp.float32)  23.3 us
  transfers between devices with their start and end apart: 9, of which 7 were waited for; matrix products, arithmetic and copies ran while one was open for 20% of the time, Pallas kernels for 0%

profile of v1, /device:TPU:0, one launch (start us, length us, event | category | flops | bytes accessed | tf_op | source)
XLA Modules:
  0.0 1054.9 jit_solution(14522875210808086761)
XLA Ops:
  16.5 5.2 select_select_fusion
  24.7 4.6 reshape.747
  47.3 3.2 gather_fusion
  51.4 4.6 reduce-window.14
  57.8 8.8 scatter_custom_fusion.3
  66.6 8.8 scatter_custom_fusion.4
  75.4 9.0 scatter_custom_fusion
  84.5 8.8 scatter_custom_fusion.1
  99.0 15.8 %scatter_custom_fusion.2 = s32[3968]{0:T(1024)S(1)} fusion(s32[3152]{0:T(1024)S(1)} %fusion.105, s32[3152]{0:T(1024)S(1)} %pad_add_fusion.1, s32[]{:T(128)} %constant.191.clone.1), kind=kCustom, calls=%fused_computation.210 | custom fusion | bytes 15876 | tf_op jit(solution)/shard_map/scatter | solution.py:39
  114.9 12.4 %gather_fusion.4 = bf16[3968,512]{1,0:T(8,128)(2,1)} fusion(bf16[1577,512]{1,0:T(8,128)(2,1)S(1)} %concatenate.76, s32[4096]{0:T(1024)S(1)} %pad_clamp_fusion.1), kind=kCustom, calls=%fused_computation.4 | custom fusion | bytes 8142336 | tf_op jit(solution)/shard_map/gather | solution.py:191
  127.3 2.9 fusion.136
  136.4 16.0 %scatter_custom_fusion.5 = f32[3968]{0:T(1024)S(1)} fusion(s32[3152]{0:T(1024)} %reshape.722, f32[3152]{0:T(1024)S(1)} %reshape.724, f32[]{:T(128)} %constant.180.clone.1), kind=kCustom, calls=%fused_computation.208 | custom fusion | bytes 16384 | tf_op jit(solution)/shard_map/scatter | solution.py:188
  152.5 4.0 fusion.1
  156.5 7.7 all-to-all-start.3
  165.8 12.4 %gather_fusion.1 = bf16[3968,512]{1,0:T(8,128)(2,1)} fusion(bf16[1577,512]{1,0:T(8,128)(2,1)S(1)} %concatenate.72, s32[4096]{0:T(1024)S(1)} %pad_clamp_fusion.1), kind=kCustom, calls=%fused_computation.1 | custom fusion | bytes 8142336 | tf_op jit(solution)/shard_map/gather | solution.py:158
  178.2 76.5 %all-to-all-done.3 = bf16[16,248,512]{2,1,0:T(8,128)(2,1)} async-done(((bf16[16,248,512]{2,1,0:T(8,128)(2,1)}), bf16[16,248,512]{2,1,0:T(8,128)(2,1)}, u32[]{:S(2)}, u32[]{:S(2)}) %all-to-all-start.3) | async-done | bytes 4063264 | tf_op jit(solution)/shard_map/all_to_all | solution.py:56
  254.7 4.6 all-to-all-start
  259.3 20.9 %gather_fusion.2 = s32[3968]{0:T(1024)S(1)} fusion(s32[1577]{0:T(1024)S(1)} %pad_add_fusion.2, s32[4096]{0:T(1024)S(1)} %pad_clamp_fusion.1), kind=kCustom, calls=%fused_computation.2 | custom fusion | bytes 47616 | tf_op jit(solution)/shard_map/gather | solution.py:160
  280.9 7.6 fusion.19
  288.5 60.5 %all-to-all-done = bf16[16,248,512]{2,1,0:T(8,128)(2,1)} async-done(((bf16[16,248,512]{2,1,0:T(8,128)(2,1)}), bf16[16,248,512]{2,1,0:T(8,128)(2,1)}, u32[]{:S(2)}, u32[]{:S(2)}) %all-to-all-start) | async-done | bytes 4063264 | tf_op jit(solution)/shard_map/all_to_all | solution.py:56
  349.0 3.6 all-to-all-start.1
  352.7 7.6 fusion.23
  360.3 3.4 fusion.39
  363.8 6.7 fusion.44
  370.5 19.2 %multiply_convert_fusion = (bf16[8,2,248,512]{3,2,0,1:T(8,128)(2,1)S(1)}, f32[8,2,248,512]{3,2,0,1:T(8,128)}) fusion(f32[8,2,248,512]{3,2,0,1:T(8,128)S(1)} %get-tuple-element.78, u8[2,248,512]{2,1,0:T(8,128)(4,1)S(1)} %get-tuple-element.25, u8[2,248,512]{2,1,0:T(8,128)(4,1)S(1)} %get-tuple-element.24), kind=kLoop, calls=%fused_computation.28 | loop fusion | flops 142213120 | bytes 20824064 | tf_op jit(solution)/shard_map/convert_element_type | solution.py:174
  389.8 4.9 fusion.41
  394.7 8.2 add_convert_fusion
  418.1 150.5 %all-reduce.19.cloned.1.call-done = (bf16[16,248,512]{2,1,0:T(8,128)(2,1)}, bf16[16,248,512]{2,1,0:T(8,128)(2,1)}) async-done(((bf16[16,248,512]{2,1,0:T(8,128)(2,1)}, bf16[16,248,512]{2,1,0:T(8,128)(2,1)}), (bf16[16,248,512]{2,1,0:T(8,128)(2,1)}, bf16[16,248,512]{2,1,0:T(8,128)(2,1)})) %all-reduce.19.cloned.1.call-update) | async-done | bytes 8126480 | tf_op jit(solution)/shard_map/psum | solution.py:63
  568.6 96.2 %all_to_all.30 = bf16[16,248,512]{2,1,0:T(8,128)(2,1)} all-to-all(bf16[16,248,512]{2,1,0:T(8,128)(2,1)} %get-tuple-element.42), channel_id=1, replica_groups=mesh['expert'=8,'tensor'=4] {'expert'}, dimensions={0} | all-to-all | bytes 8126464 | tf_op jit(solution)/shard_map/all_to_all | solution.py:64
  664.9 4.7 all-to-all-start.4
  672.9 4.1 convolution_bitcast_fusion.1
  679.0 3.7 fusion.64
  682.7 4.1 fusion.61
  686.8 13.5 %gather_fusion.3 = bf16[3152,512]{1,0:T(8,128)(2,1)} fusion(bf16[3968,512]{1,0:T(8,128)(2,1)} %bitcast.214, s32[4096]{0:T(1024)S(1)} %pad_clamp_fusion), kind=kCustom, calls=%fused_computation.3 | custom fusion | bytes 6467904 | tf_op jit(solution)/shard_map/gather | solution.py:183
  700.3 7.9 reshape.734
  708.1 21.8 %multiply_reduce_fusion = (f32[1576,2]{1,0:T(8,128)}, f32[1576,512]{1,0:T(8,128)}) fusion(f32[1576,2,512]{2,1,0:T(2,128)} %reshape.734, f32[1576,512]{1,0:T(8,128)} %convert_element_type.195, f32[1576,2]{1,0:T(8,128)S(1)} %copy.191), kind=kLoop, calls=%fused_computation.41 | loop fusion | flops 5645232 | bytes 12935808 | tf_op jit(solution)/shard_map/reduce_sum | solution.py:186
  731.5 27.2 %all-to-all-done.4 = bf16[16,248,512]{2,1,0:T(8,128)(2,1)} async-done(((bf16[16,248,512]{2,1,0:T(8,128)(2,1)}), bf16[16,248,512]{2,1,0:T(8,128)(2,1)}, u32[]{:S(2)}, u32[]{:S(2)}) %all-to-all-start.4) | async-done | bytes 4063264 | tf_op jit(solution)/shard_map/all_to_all | solution.py:64
  758.7 13.1 %gather_fusion.5 = bf16[3152,512]{1,0:T(8,128)(2,1)} fusion(bf16[3968,512]{1,0:T(8,128)(2,1)} %bitcast.41, s32[4096]{0:T(1024)S(1)} %pad_clamp_fusion), kind=kCustom, calls=%fused_computation.5 | custom fusion | bytes 6467904 | tf_op jit(solution)/shard_map/gather | solution.py:219
  771.8 7.9 reshape.735
  780.6 35.1 %multiply_reduce_fusion.1 = f32[1576,512]{1,0:T(8,128)S(1)} fusion(f32[1576,2,512]{2,1,0:T(2,128)} %reshape.735, f32[1576,2]{1,0:T(8,128)S(1)} %copy.207), kind=kLoop, calls=%fused_computation.42 | loop fusion | flops 2420736 | bytes 9695552 | tf_op jit(solution)/shard_map/reduce_sum | solution.py:219
  827.2 3.1 multiply_reduce_fusion.3
  835.6 3.1 convert_element_type.211
  844.8 4.0 fusion.30
  852.4 4.4 fusion.143
  856.8 20.1 %all-reduce.17.cloned.1.call-done = (f32[512,128]{1,0:T(8,128)}, f32[512,128]{1,0:T(8,128)}, f32[128,512]{1,0:T(8,128)}) async-done(((f32[512,128]{1,0:T(8,128)}, f32[512,128]{1,0:T(8,128)}, f32[128,512]{1,0:T(8,128)}), (f32[512,128]{1,0:T(8,128)}, f32[512,128]{1,0:T(8,128)}, f32[128,512]{1,0:T(8,128)})) %all-reduce.17.cloned.1.call-update) | async-done | bytes 786448 | tf_op jit(solution)/shard_map/psum | solution.py:296
  877.5 22.4 %psum.137 = f32[128,16]{0,1:T(8,128)} all-reduce(f32[128,16]{0,1:T(8,128)S(1)} %fusion.144), channel_id=1, replica_groups=mesh['expert'=8,'tensor'=4] {'expert'}, use_global_device_ids=true, to_apply=%region_39.40 | all-reduce | flops 2048 | bytes 16384 | tf_op jit(solution)/shard_map/psum | solution.py:283
  900.0 23.3 %all-reduce.13.cloned.1.call-done = bf16[1576,512]{1,0:T(8,128)(2,1)} async-done(((bf16[1576,512]{1,0:T(8,128)(2,1)}), bf16[1576,512]{1,0:T(8,128)(2,1)}) %all-reduce.13.cloned.1.call-update) | async-done | bytes 1613840 | tf_op jit(solution)/shard_map/psum | solution.py:273
  931.5 103.6 %all-reduce.15.cloned.1.call-done = (f32[512,128]{1,0:T(8,128)}, f32[128,3,128]{2,0,1:T(8,128)}, f32[128,128]{1,0:T(8,128)}, f32[128,512]{1,0:T(8,128)}, f32[512...) async-done(((f32[512,128]{1,0:T(8,128)}, f32[128,3,128]{2,0,1:T(8,128)}, f32[128,128]{1,0:T(8,128)}, ...) | async-done | bytes 2097168 | tf_op jit(solution)/shard_map/psum | solution.py:295
  (360 shorter events, 117.4 us)
Async XLA Ops:
  7.2 345.5 %copy-start = (bf16[2,512,512]{2,1,0:T(8,128)(2,1)S(1)}, bf16[2,512,512]{2,1,0:T(8,128)(2,1)}, u32[]{:S(2)}) copy-start(bf16[2,512,512]{2,1,0:T(8,128)(2,1)} %param.30) | copy-start | bytes 3145732
  7.2 7.5 copy-start.6
  7.2 6.1 copy-start.52
  7.2 7.5 copy-start.84
  7.2 120.0 %all-reduce.21.cloned.1.call-start = ((), (), s32[]{:S(2)}) async-start(), calls=%async_computation.9 | async-start | bytes 4034560 | tf_op jit(solution)/shard_map/psum | solution.py:140
  7.3 14.4 %copy-start.90 = (s32[128]{0:T(128)}, s32[128]{0:T(128)S(1)}, u32[]{:S(2)}) copy-start(s32[128]{0:T(128)S(1)} %and_select_fusion) | copy-start | bytes 1540
  10.6 5.8 copy-start.55
  14.7 7.7 copy-start.53
  15.3 6.4 copy-start.9
  15.4 6.4 copy-start.64
  34.5 6.1 copy-start.27
  114.9 12.4 %copy-start.68 = (bf16[128,512]{1,0:T(8,128)(2,1)S(1)}, bf16[128,512]{1,0:T(8,128)(2,1)}, u32[]{:S(2)}) copy-start(bf16[128,512]{1,0:T(8,128)(2,1)} %param.35) | copy-start | bytes 393220
  114.9 12.4 %copy-start.91 = (s32[128]{0:T(128)S(1)}, s32[128]{0:T(128)}, u32[]{:S(2)}) copy-start(s32[128]{0:T(128)} %copy-done.90) | copy-start | bytes 1540
  156.5 98.1 %all-to-all-start.3 = ((bf16[16,248,512]{2,1,0:T(8,128)(2,1)}), bf16[16,248,512]{2,1,0:T(8,128)(2,1)}, u32[]{:S(2)}, u32[]{:S(2)}) async-start(bf16[16,248,512]{2,1,0:T(8,128)(2,1)} %fusion.1), calls=%async_computation.3 | async-start | bytes 8126464 | tf_op jit(solution)/shard_map/all_to_all | solution.py:56
  254.7 94.3 %all-to-all-start = ((bf16[16,248,512]{2,1,0:T(8,128)(2,1)}), bf16[16,248,512]{2,1,0:T(8,128)(2,1)}, u32[]{:S(2)}, u32[]{:S(2)}) async-start(bf16[16,248,512]{2,1,0:T(8,128)(2,1)} %bitcast.219), calls=%async_computation | async-start | bytes 8126464 | tf_op jit(solution)/shard_map/all_to_all | solution.py:56
  259.3 21.6 %copy-start.31 = (bf16[2,512,512]{2,1,0:T(8,128)(2,1)S(1)}, bf16[2,512,512]{2,1,0:T(8,128)(2,1)}, u32[]{:S(2)}) copy-start(bf16[2,512,512]{2,1,0:T(8,128)(2,1)} %param.31) | copy-start | bytes 3145732
  349.0 11.3 %all-to-all-start.1 = ((s32[8,2,248]{2,1,0:T(2,128)}), s32[8,2,248]{2,1,0:T(2,128)S(1)}, u32[]{:S(2)}, u32[]{:S(2)}) async-start(s32[8,2,248]{2,1,0:T(2,128)} %all_to_all.20), calls=%async_computation.1 | async-start | bytes 32768 | tf_op jit(solution)/shard_map/all_to_all | solution.py:57
  352.6 216.0 %all-reduce.19.cloned.1.call-start = ((), (), s32[]{:S(2)}) async-start(), calls=%async_computation.8 | async-start | bytes 16252928 | tf_op jit(solution)/shard_map/psum | solution.py:63
  352.7 7.6 copy-start.59
  352.7 7.6 copy-start.92
  363.7 6.8 copy-start.43
  363.7 30.9 %slice-start = ((s8[8126464]{0:T(1024)(128)(4,1)}), s8[4194304]{0:T(1024)(128)(4,1)S(1)}, s32[]{:S(2)}) async-start(s8[8126464]{0:T(1024)(128)(4,1)} %bitcast.220), calls=%async_computation.10 | async-start | bytes 8388608
  370.5 19.2 %copy-start.22 = (f32[8,2,248,512]{3,2,0,1:T(8,128)}, f32[8,2,248,512]{3,2,0,1:T(8,128)S(1)}, u32[]{:S(2)}) copy-start(f32[8,2,248,512]{3,2,0,1:T(8,128)S(1)} %get-tuple-element.78) | copy-start | bytes 24379396
  370.5 19.2 %copy-start.61 = (bf16[128,512]{1,0:T(8,128)(2,1)S(1)}, bf16[128,512]{1,0:T(8,128)(2,1)}, u32[]{:S(2)}) copy-start(bf16[128,512]{1,0:T(8,128)(2,1)} %param.41) | copy-start | bytes 393220
  370.5 24.1 %slice-start.1 = ((s8[8126464]{0:T(1024)(128)(4,1)}), s8[3932160]{0:T(1024)(128)(4,1)S(1)}, s32[]{:S(2)}) async-start(s8[8126464]{0:T(1024)(128)(4,1)} %bitcast.220), calls=%async_computation.11 | async-start | bytes 7864320
  389.8 23.2 %copy-start.15 = (bf16[8,2,248,512]{3,2,0,1:T(8,128)(2,1)}, bf16[8,2,248,512]{3,2,0,1:T(8,128)(2,1)S(1)}, u32[]{:S(2)}) copy-start(bf16[8,2,248,512]{3,2,0,1:T(8,128)(2,1)S(1)} %get-tuple-element.50) | copy-start | bytes 12189700
  394.6 8.2 copy-start.103
  664.9 93.8 %all-to-all-start.4 = ((bf16[16,248,512]{2,1,0:T(8,128)(2,1)}), bf16[16,248,512]{2,1,0:T(8,128)(2,1)}, u32[]{:S(2)}, u32[]{:S(2)}) async-start(bf16[16,248,512]{2,1,0:T(8,128)(2,1)} %get-tuple-element.43), calls=%async_computation.4 | async-start | bytes 8126464 | tf_op jit(solution)/shard_map/all_to_all | solution.py:64
  669.6 207.4 %all-reduce.17.cloned.1.call-start = ((), (), s32[]{:S(2)}) async-start(), calls=%async_computation.7 | async-start | bytes 1572864 | tf_op jit(solution)/shard_map/psum | solution.py:296
  708.1 23.2 %copy-start.73 = (f32[1576,2]{0,1:T(2,128)S(1)}, f32[1576,2]{0,1:T(2,128)}, u32[]{:S(2)}) copy-start(f32[1576,2]{0,1:T(2,128)} %get-tuple-element.49) | copy-start | bytes 37828
  708.1 23.3 %copy-start.72 = (s32[1576,2]{0,1:T(2,128)S(1)}, s32[1576,2]{0,1:T(2,128)}, u32[]{:S(2)}) copy-start(s32[1576,2]{0,1:T(2,128)} %param.43) | copy-start | bytes 37828
  731.5 84.2 %copy-start.36 = (f32[1576,16]{0,1:T(8,128)}, f32[1576,16]{0,1:T(8,128)S(1)}, u32[]{:S(2)}) copy-start(f32[1576,16]{0,1:T(8,128)S(1)} %select_reduce_fusion) | copy-start | bytes 302596
  771.8 7.9 copy-start.93
  780.6 35.1 %copy-start.79 = (bf16[512,16]{0,1:T(8,128)(2,1)S(1)}, bf16[512,16]{0,1:T(8,128)(2,1)}, u32[]{:S(2)}) copy-start(bf16[512,16]{0,1:T(8,128)(2,1)} %param.29) | copy-start | bytes 49156
  833.5 5.8 copy-start.33
  843.5 79.7 %all-reduce.13.cloned.1.call-start = ((), (), s32[]{:S(2)}) async-start(), calls=%async_computation.5 | async-start | bytes 3227648 | tf_op jit(solution)/shard_map/psum | solution.py:273
  848.9 186.3 %all-reduce.15.cloned.1.call-start = ((), (), s32[]{:S(2)}) async-start(), calls=%async_computation.6 | async-start | bytes 4194304 | tf_op jit(solution)/shard_map/psum | solution.py:295
  849.8 27.1 %copy-start.24 = (f32[1576,128]{1,0:T(8,128)S(1)}, f32[1576,128]{1,0:T(8,128)}, u32[]{:S(2)}) copy-start(f32[1576,128]{1,0:T(8,128)} %copy-done.23) | copy-start | bytes 2420740
  849.8 27.1 %copy-start.37 = (f32[1576,16]{0,1:T(8,128)S(1)}, f32[1576,16]{0,1:T(8,128)}, u32[]{:S(2)}) copy-start(f32[1576,16]{0,1:T(8,128)} %copy-done.36) | copy-start | bytes 302596
  852.4 70.8 %copy-start.7 = (bf16[1576,512]{1,0:T(8,128)(2,1)S(1)}, bf16[1576,512]{1,0:T(8,128)(2,1)}, u32[]{:S(2)}) copy-start(bf16[1576,512]{1,0:T(8,128)(2,1)} %param.24) | copy-start | bytes 4841476
  852.4 70.8 %copy-start.56 = (f32[1576]{0:T(1024)S(1)}, f32[1576]{0:T(1024)}, u32[]{:S(2)}) copy-start(f32[1576]{0:T(1024)} %copy-done.55) | copy-start | bytes 18916
  852.4 70.8 %copy-start.85 = (f32[512]{0:T(512)S(1)}, f32[512]{0:T(512)}, u32[]{:S(2)}) copy-start(f32[512]{0:T(512)} %param.25) | copy-start | bytes 6148
  856.8 69.0 %copy-start.75 = (f32[1576]{0:T(1024)S(1)}, f32[1576]{0:T(1024)}, u32[]{:S(2)}) copy-start(f32[1576]{0:T(1024)} %copy-done.74) | copy-start | bytes 18916
  856.8 69.0 %copy-start.63 = (f32[1576]{0:T(1024)S(1)}, f32[1576]{0:T(1024)}, u32[]{:S(2)}) copy-start(f32[1576]{0:T(1024)} %copy-done.62) | copy-start | bytes 18916
  923.3 5.4 copy-start.14
  928.7 119.3 %copy-start.1 = (bf16[2,512,512]{2,1,0:T(8,128)(2,1)S(1)}, bf16[2,512,512]{2,1,0:T(8,128)(2,1)}, u32[]{:S(2)}) copy-start(bf16[2,512,512]{2,1,0:T(8,128)(2,1)} %param.30) | copy-start | bytes 3145732
  1035.1 11.5 %copy-start.58 = (f32[512,128]{1,0:T(8,128)S(1)}, f32[512,128]{1,0:T(8,128)}, u32[]{:S(2)}) copy-start(f32[512,128]{1,0:T(8,128)} %get-tuple-element.93) | copy-start | bytes 786436
  1035.2 12.2 %copy-start.57 = (f32[128,512]{1,0:T(8,128)S(1)}, f32[128,512]{1,0:T(8,128)}, u32[]{:S(2)}) copy-start(f32[128,512]{1,0:T(8,128)} %get-tuple-element.94) | copy-start | bytes 786436
  (68 other events, 166.3 us)
Sparse Core Ops, SparseCore 0:
  47.1 53.0 all-reduce.20
  418.3 150.3 all-reduce.18
  843.7 33.2 all-reduce.16
  879.3 43.9 all-reduce.12
  929.0 106.0 all-reduce.14
